TPU v7x, 32 devices: a whole 2x2x4 slice. The times are simulated.
32 devices in a mesh: row: 8 (over z, y), col: 4 (over x, core).
Axes of the slice: x: 2, y: 2, z: 4, core: 2. Of those that a mesh axis runs over, the one named last changes fastest.
Arguments:
- weights: float32 [192, 16, 64, 64], P('row', 'col'), may hold values from 9.765625e-05 to 0.0029296875
- block_cols: int32 [192, 16], P('row'), may hold values from 0 to 191, as said below
- counts: int32 [192], P('row'), may hold values from 1 to 16, as said below
- near_null: float32 [192, 64], P('row'), may hold values from 0.5 to 2
- prior_ridge: float32 [192, 64], P('row'), may hold values from 0.1 to 1
Outputs:
- coarse_band: float32 [192, 128], P(('row', 'col'))
Inputs may be any that keep to these rules, and one draw needn't show every extreme that they name: `block_cols`: row i holds i in slot 0; its other slots hold distinct aggregates j with (j - i) modulo 192 between -21 and 21 and not 0; some row holds a neighbour at +21 and some at -21. Slots at or beyond a row's count are unused. `counts`: both ends are reached in every draw; the mean over the 24 rows of one index of row differs from index to index.
All inputs are finite; a program needn't handle non-finite values.
Results may differ from a plain program's by a relative error of at most 0.0003.
Values sent between devices are 32-bit elements; how exact they have to be, the bound alone decides.
No kernel may reach another device: no remote copies, remote signals or barrier semaphores. Data moves between devices by JAX's collectives and lax.ppermute only.
A program may use at most 64 MiB of HBM per device.

v0:
```python
import jax
import jax.numpy as jnp
from jax import lax
from jax.sharding import PartitionSpec as P

H = 21
BAND = 128
epsilon = 1e-06
relax_weight = 2.0 / 3.0


def with_halo(block, sides, width):
    for axis, dim in sides:
        count = lax.axis_size(axis)
        forward = [(i, i + 1) for i in range(count - 1)]
        forward.append((count - 1, 0))
        backward = [(target, source) for source, target in forward]
        low = lax.ppermute(
            lax.slice_in_dim(block, block.shape[dim] - width, None, axis=dim), axis, forward
        )
        high = lax.ppermute(lax.slice_in_dim(block, 0, width, axis=dim), axis, backward)
        block = jnp.concatenate([low, block, high], axis=dim)
    return block


def shifted_2(array, axis, by):
    devices = lax.axis_size(axis)
    return lax.ppermute(array, axis, [(i, (i + by) % devices) for i in range(devices)])


def band_form(tiles, tile_offsets):
    one_hot = (
        tile_offsets[..., None] + BAND // 2 == jnp.arange(BAND, dtype=jnp.int32)[None, None, :]
    ).astype(jnp.float32)
    return jnp.einsum("nkx,nkq->nxq", tiles, one_hot, precision=lax.Precision.HIGHEST)


def shift_table(amounts):
    band_pos = jnp.arange(BAND, dtype=jnp.int32)
    source = (band_pos[None, None, :] - amounts[:, None, None]) % BAND
    return (band_pos[None, :, None] == source).astype(jnp.float32)


def on_device(weights, block_cols, counts, near_null, prior_ridge):
    highest = lax.Precision.HIGHEST
    block_rows = weights.shape[0]
    slot_count = weights.shape[1]
    all_slots = block_cols.shape[1]
    total_blocks = block_rows * lax.axis_size("row")
    first_block = lax.axis_index("row") * block_rows
    column = lax.axis_index("col")
    local_rows = jnp.arange(block_rows, dtype=jnp.int32)
    offsets = (block_cols - (first_block + local_rows)[:, None] + H) % total_blocks - H
    mask_all = (jnp.arange(all_slots, dtype=jnp.int32)[None, :] < counts[:, None]).astype(
        jnp.float32
    )
    slot_start = column * slot_count
    mask_own = lax.dynamic_slice_in_dim(mask_all, slot_start, slot_count, 1)
    own_offsets = lax.dynamic_slice_in_dim(offsets, slot_start, slot_count, 1)
    slot_ids = slot_start + jnp.arange(slot_count, dtype=jnp.int32)
    degree_part = jnp.einsum("ikxy,ik->ix", weights, mask_own, precision=highest)
    degree = lax.psum(degree_part, "col") + prior_ridge
    unit_null = near_null / jnp.sqrt(
        jnp.sum(near_null * near_null, axis=1, keepdims=True) + epsilon
    )
    null_ext = with_halo(unit_null, (("row", 0),), H)
    targets = local_rows[:, None] + H + own_offsets
    near_rows = null_ext[targets]
    applied = jnp.einsum("ikxy,iky->ikx", weights, near_rows, precision=highest)
    own_term = (
        jnp.where(slot_ids == 0, 1.0 - relax_weight, 0.0).astype(jnp.float32)[None, :, None]
        * unit_null[:, None, :]
    )
    prolong = mask_own[:, :, None] * (own_term + relax_weight * applied / degree[:, None, :])
    part_band = band_form(prolong, own_offsets)
    whole_band = lax.psum(part_band, "col")
    ext_band = with_halo(whole_band, (("row", 0),), H)
    pick_hot = (
        offsets[..., None] + BAND // 2 == jnp.arange(BAND, dtype=jnp.int32)[None, None, :]
    ).astype(jnp.float32)
    full_slots = jnp.einsum("ixq,ikq->ikx", whole_band, pick_hot, precision=highest)
    own_band = ext_band[H : H + block_rows]
    summed = jnp.zeros(own_band.shape, jnp.float32)
    for slot_index in range(slot_count):
        picked = ext_band[targets[:, slot_index]]
        mover = shift_table(own_offsets[:, slot_index])
        rolled = jnp.einsum("iyp,ipq->iyq", picked, mover, precision=highest)
        step_term = jnp.einsum("ixy,iyq->ixq", weights[:, slot_index], rolled, precision=highest)
        summed = summed + mask_own[:, slot_index][:, None, None] * step_term
    applied_p = jnp.where(column == 0, degree[:, :, None] * own_band, 0.0) - summed
    contrib = jnp.einsum("ikx,ixq->ikq", full_slots, applied_p, precision=highest)
    pieces = []
    for slot_index in range(all_slots):
        mover = shift_table(-offsets[:, slot_index])
        pieces.append(jnp.einsum("ip,ipq->iq", contrib[:, slot_index], mover, precision=highest))
    shifted = jnp.stack(pieces, axis=1)
    destination = (local_rows[:, None] + H + offsets).reshape(-1)
    one_hot = (
        destination[:, None] == jnp.arange(block_rows + 2 * H, dtype=jnp.int32)[None, :]
    ).astype(jnp.float32)
    collected = jnp.einsum("nt,nq->tq", one_hot, shifted.reshape(-1, BAND), precision=highest)
    from_prev = shifted_2(collected[block_rows + H :], "row", 1)
    from_next = shifted_2(collected[:H], "row", -1)
    own_coarse = collected[H : block_rows + H]
    own_coarse = own_coarse.at[:H].add(from_prev)
    own_coarse = own_coarse.at[block_rows - H :].add(from_next)
    return lax.psum_scatter(own_coarse, "col", scatter_dimension=0, tiled=True)


def solution(mesh):
    placed = (P("row", "col", None, None), P("row", None), P("row"), P("row", None), P("row", None))
    return jax.shard_map(
        on_device, mesh=mesh, in_specs=placed, out_specs=P(("row", "col"), None), check_vma=False
    )
```

profile of v0, /device:TPU:0, one launch (start us, length us, event | category | flops | bytes accessed | tf_op | source)
XLA Modules:
  0.0 173.7 jit_solution(2995312101073054942)
XLA Ops:
  6.5 0.8 multiply_reduce_fusion
  8.2 3.0 %collective-permute-start = (f32[21,64]{1,0:T(8,128)S(1)}, f32[21,64]{1,0:T(8,128)S(1)}, u32[]{:S(2)}, u32[]{:S(2)}) collective-permute-start(f32[21,64]{1,0:T(8,128)S(1)} %get-tuple-element.39), channel_id=1, source_target_pairs={{0,4},{4,8},{8,12},{12,16},{16,20},{20,24},{24,28},{28,0},{1,5},{5... | collective-permute-start | bytes 16136 | tf_op jit(solution)/shard_map/ppermute | solution.py:18
  11.2 3.1 %collective-permute-start.1 = (f32[21,64]{1,0:T(8,128)S(1)}, f32[21,64]{1,0:T(8,128)S(1)}, u32[]{:S(2)}, u32[]{:S(2)}) collective-permute-start(f32[21,64]{1,0:T(8,128)S(1)} %get-tuple-element.40), channel_id=1, source_target_pairs={{4,0},{8,4},{12,8},{16,12},{20,16},{24,20},{28,24},{0,28},{5,1},{9... | collective-permute-start | bytes 16136 | tf_op jit(solution)/shard_map/ppermute | solution.py:21
  21.9 2.9 %reduce_sum.19 = f32[24,4,64]{2,1,0:T(4,128)S(1)} reduce(f32[24,4,64,64]{3,2,1,0:T(8,128)} %param.9, f32[]{:T(128)} %constant.208.clone.1), dimensions={3}, to_apply=%region_1.2 | reduce | flops 387072 | bytes 1597444 | tf_op jit(solution)/shard_map/ikxy,ik->ix/reduce_sum | solution.py:61
  25.1 10.6 %psum.14 = f32[24,64]{1,0:T(8,128)S(1)} all-reduce(f32[24,64]{1,0:T(8,128)S(1)} %bitcast.240), channel_id=1, replica_groups=mesh['row'=8,'col'=4] {'col'}, use_global_device_ids=true, to_apply=%region_2.3 | all-reduce | flops 1536 | bytes 12288 | tf_op jit(solution)/shard_map/psum | solution.py:62
  36.4 5.0 %fusion.175 = f32[24,4,1,64]{3,2,1,0:T(1,128)S(1)} fusion(f32[24,4,64,1]{2,3,1,0:T(1,128)S(1)} %bitcast.239, f32[24,4,64,64]{3,2,1,0:T(8,128)S(1)} %copy-done), kind=kOutput, calls=%fused_computation.338 | convolution fusion | flops 4718592 | bytes 1622016 | tf_op jit(solution)/shard_map/ikxy,iky->ikx/dot_general | solution.py:69
  41.4 1.8 %fusion.57 = f32[24,64,128]{2,1,0:T(8,128)} fusion(f32[24,4,64]{2,1,0:T(4,128)S(1)} %bitcast.238, s32[24,4]{1,0:T(8,128)S(1)} %copy.19, f32[24,64]{1,0:T(8,128)S(1)} %add.346, f32[24,64]{1,0:T(8,128)S(1)} %broadcast_divide_fusion, f32[4]{0:T(128)S(1)} %copy-done.16, f32[24,4]{1,0:T(8,128)S(1)} %copy.17), kind=kOutput, calls=%fused_computation.90 | convolution fusion | flops 9480192 | bytes 824080 | tf_op jit(solution)/shard_map/nkx,nkq->nxq/dot_general | solution.py:35
  44.5 32.1 %all-reduce.3.cloned.1.call-done = f32[24,64,128]{2,1,0:T(8,128)} async-done(((f32[24,64,128]{2,1,0:T(8,128)}), f32[24,64,128]{2,1,0:T(8,128)}) %all-reduce.3.cloned.1.call-update) | async-done | bytes 786448 | tf_op jit(solution)/shard_map/psum | solution.py:76
  76.6 1.5 fusion.172
  78.0 1.5 collective-permute-start.2
  80.2 3.2 %collective-permute-start.3 = (f32[21,64,128]{2,1,0:T(8,128)S(1)}, f32[21,64,128]{2,1,0:T(8,128)S(1)}, u32[]{:S(2)}, u32[]{:S(2)}) collective-permute-start(f32[21,64,128]{2,1,0:T(8,128)S(1)} %get-tuple-element.35), channel_id=1, source_target_pairs={{4,0},{8,4},{12,8},{16,12},{20,16},{24,20},{28,24},{0,28},{5,1},{9... | collective-permute-start | bytes 2064392 | tf_op jit(solution)/shard_map/ppermute | solution.py:21
  84.8 23.1 %collective-permute-done.2 = f32[21,64,128]{2,1,0:T(8,128)S(1)} collective-permute-done((f32[21,64,128]{2,1,0:T(8,128)S(1)}, f32[21,64,128]{2,1,0:T(8,128)S(1)}, u32[]{:S(2)}, u32[]{:S(2)}) %collective-permute-start.2) | collective-permute-done | bytes 688160 | tf_op jit(solution)/shard_map/ppermute | solution.py:18
  107.9 0.9 constant_dynamic-update-slice_fusion.2
  108.8 1.0 constant_dynamic-update-slice_fusion.1
  109.8 1.0 collective-permute-done.3
  110.8 0.9 constant_dynamic-update-slice_fusion
  111.7 3.2 %gather_fusion.1 = f32[24,64,128]{2,1,0:T(8,128)} fusion(f32[66,64,128]{2,1,0:T(8,128)} %constant_dynamic-update-slice_fusion, s32[1024]{0:T(1024)} %pad_clamp_fusion.3), kind=kCustom, calls=%fused_computation.1 | custom fusion | bytes 1572960 | tf_op jit(solution)/shard_map/gather | solution.py:85
  114.9 3.2 %gather_fusion.2 = f32[24,64,128]{2,1,0:T(8,128)} fusion(f32[66,64,128]{2,1,0:T(8,128)} %constant_dynamic-update-slice_fusion, s32[1024]{0:T(1024)} %pad_clamp_fusion.2), kind=kCustom, calls=%fused_computation.2 | custom fusion | bytes 1572960 | tf_op jit(solution)/shard_map/gather | solution.py:85
  118.1 3.2 %gather_fusion.3 = f32[24,64,128]{2,1,0:T(8,128)} fusion(f32[66,64,128]{2,1,0:T(8,128)} %constant_dynamic-update-slice_fusion, s32[1024]{0:T(1024)} %pad_clamp_fusion.1), kind=kCustom, calls=%fused_computation.3 | custom fusion | bytes 1572960 | tf_op jit(solution)/shard_map/gather | solution.py:85
  121.4 3.2 %gather_fusion.4 = f32[24,64,128]{2,1,0:T(8,128)} fusion(f32[66,64,128]{2,1,0:T(8,128)} %constant_dynamic-update-slice_fusion, s32[1024]{0:T(1024)} %pad_clamp_fusion), kind=kCustom, calls=%fused_computation.4 | custom fusion | bytes 1572960 | tf_op jit(solution)/shard_map/gather | solution.py:85
  124.6 2.1 %fusion = f32[24,64,128]{2,1,0:T(8,128)S(1)} fusion(f32[24,64,128]{2,1,0:T(8,128)} %gather_fusion.1, s32[24,128]{1,0:T(8,128)S(1)} %add_select_fusion.19), kind=kOutput, calls=%fused_computation.25 | convolution fusion | flops 302383104 | bytes 1585152 | tf_op jit(solution)/shard_map/iyp,ipq->iyq/dot_general | solution.py:87
  126.7 0.9 convolution_multiply_fusion.3
  127.8 0.9 fusion.1
  128.7 0.9 fusion.2
  129.7 0.9 fusion.3
  130.6 0.9 fusion.24
  131.5 0.9 fusion.23
  132.7 1.0 fusion.22
  134.5 0.8 fusion.10
  135.3 0.8 fusion.11
  136.1 0.8 fusion.12
  136.9 1.0 fusion.13
  138.0 0.8 fusion.14
  138.8 0.8 fusion.15
  139.6 0.8 fusion.16
  140.4 0.8 fusion.17
  141.2 0.8 fusion.18
  142.0 0.8 fusion.19
  142.9 0.8 fusion.6
  143.7 0.8 fusion.7
  144.5 0.8 fusion.8
  145.3 0.8 fusion.9
  146.1 0.8 fusion.5
  146.9 0.8 fusion.4
  148.5 1.5 collective-permute-start.4
  151.3 3.3 %collective-permute-start.5 = (f32[21,128]{1,0:T(8,128)S(1)}, f32[21,128]{1,0:T(8,128)S(1)}, u32[]{:S(2)}, u32[]{:S(2)}) collective-permute-start(f32[21,128]{1,0:T(8,128)S(1)} %get-tuple-element.37), channel_id=1, source_target_pairs={{0,28},{4,0},{8,4},{12,8},{16,12},{20,16},{24,20},{28,24},{1,29},{... | collective-permute-start | bytes 32264 | tf_op jit(solution)/shard_map/ppermute | solution.py:28
  155.1 0.8 collective-permute-done.5
  156.2 10.1 %all-reduce = f32[24,128]{1,0:T(8,128)S(1)} all-reduce(f32[24,128]{1,0:T(8,128)S(1)} %scatter-add.9), channel_id=2, replica_groups=mesh['row'=8,'col'=4] {'col'}, use_global_device_ids=true, to_apply=%region_4.5.clone | all-reduce | flops 3072 | bytes 24576
  (104 shorter events, 16.6 us)
Async XLA Ops:
  6.5 70.0 %all-reduce.3.cloned.1.call-start = ((), (), s32[]{:S(2)}) async-start(), calls=%async_computation | async-start | bytes 1572864 | tf_op jit(solution)/shard_map/psum | solution.py:76
  8.2 27.5 %collective-permute-start = (f32[21,64]{1,0:T(8,128)S(1)}, f32[21,64]{1,0:T(8,128)S(1)}, u32[]{:S(2)}, u32[]{:S(2)}) collective-permute-start(f32[21,64]{1,0:T(8,128)S(1)} %get-tuple-element.39), channel_id=1, source_target_pairs={{0,4},{4,8},{8,12},{12,16},{16,20},{20,24},{24,28},{28,0},{1,5},{5... | collective-permute-start | bytes 16136 | tf_op jit(solution)/shard_map/ppermute | solution.py:18
  11.2 24.5 %collective-permute-start.1 = (f32[21,64]{1,0:T(8,128)S(1)}, f32[21,64]{1,0:T(8,128)S(1)}, u32[]{:S(2)}, u32[]{:S(2)}) collective-permute-start(f32[21,64]{1,0:T(8,128)S(1)} %get-tuple-element.40), channel_id=1, source_target_pairs={{4,0},{8,4},{12,8},{16,12},{20,16},{24,20},{28,24},{0,28},{5,1},{9... | collective-permute-start | bytes 16136 | tf_op jit(solution)/shard_map/ppermute | solution.py:21
  21.9 13.8 %copy-start.11 = (f32[24,64]{1,0:T(8,128)S(1)}, f32[24,64]{1,0:T(8,128)}, u32[]{:S(2)}) copy-start(f32[24,64]{1,0:T(8,128)} %param.13) | copy-start | bytes 18436
  21.9 14.4 %copy-start = (f32[24,4,64,64]{3,2,1,0:T(8,128)S(1)}, f32[24,4,64,64]{3,2,1,0:T(8,128)}, u32[]{:S(2)}) copy-start(f32[24,4,64,64]{3,2,1,0:T(8,128)} %param.9) | copy-start | bytes 4718596
  36.4 5.0 %copy-start.16 = (f32[4]{0:T(128)S(1)}, f32[4]{0:T(128)}, u32[]{:S(2)}) copy-start(f32[4]{0:T(128)} %compare_select_fusion.5) | copy-start | bytes 52
  76.6 7.5 %copy-start.1 = (f32[24,64,128]{2,1,0:T(8,128)S(1)}, f32[24,64,128]{2,1,0:T(8,128)}, u32[]{:S(2)}) copy-start(f32[24,64,128]{2,1,0:T(8,128)} %all-reduce.3.cloned.1.call-done) | copy-start | bytes 2359300
  78.0 29.9 %collective-permute-start.2 = (f32[21,64,128]{2,1,0:T(8,128)S(1)}, f32[21,64,128]{2,1,0:T(8,128)S(1)}, u32[]{:S(2)}, u32[]{:S(2)}) collective-permute-start(f32[21,64,128]{2,1,0:T(8,128)S(1)} %get-tuple-element.36), channel_id=1, source_target_pairs={{0,4},{4,8},{8,12},{12,16},{16,20},{20,24},{24,28},{28,0},{1,5},{5... | collective-permute-start | bytes 2064392 | tf_op jit(solution)/shard_map/ppermute | solution.py:18
  80.2 30.5 %collective-permute-start.3 = (f32[21,64,128]{2,1,0:T(8,128)S(1)}, f32[21,64,128]{2,1,0:T(8,128)S(1)}, u32[]{:S(2)}, u32[]{:S(2)}) collective-permute-start(f32[21,64,128]{2,1,0:T(8,128)S(1)} %get-tuple-element.35), channel_id=1, source_target_pairs={{4,0},{8,4},{12,8},{16,12},{20,16},{24,20},{28,24},{0,28},{5,1},{9... | collective-permute-start | bytes 2064392 | tf_op jit(solution)/shard_map/ppermute | solution.py:21
  121.4 5.3 %copy-start.13 = (f32[24]{0:T(128)S(1)}, f32[24]{0:T(128)}, u32[]{:S(2)}) copy-start(f32[24]{0:T(128)} %get-tuple-element.61) | copy-start | bytes 292
  126.6 1.1 copy-start.5
  126.6 2.1 %copy-start.4 = (f32[24,64,128]{2,1,0:T(8,128)S(1)}, f32[24,64,128]{2,1,0:T(8,128)}, u32[]{:S(2)}) copy-start(f32[24,64,128]{2,1,0:T(8,128)} %gather_fusion.3) | copy-start | bytes 2359300
  127.8 1.9 %copy-start.3 = (f32[24,64,128]{2,1,0:T(8,128)S(1)}, f32[24,64,128]{2,1,0:T(8,128)}, u32[]{:S(2)}) copy-start(f32[24,64,128]{2,1,0:T(8,128)} %gather_fusion.4) | copy-start | bytes 2359300
  128.7 1.9 %copy-start.15 = (f32[24]{0:T(128)S(1)}, f32[24]{0:T(128)}, u32[]{:S(2)}) copy-start(f32[24]{0:T(128)} %get-tuple-element.60) | copy-start | bytes 292
  130.6 0.9 copy-start.14
  131.5 1.1 copy-start.2
  131.5 1.1 copy-start.12
  138.8 4.9 %copy-start.6 = (s32[24,128]{1,0:T(8,128)S(1)}, s32[24,128]{1,0:T(8,128)}, u32[]{:S(2)}) copy-start(s32[24,128]{1,0:T(8,128)} %add_select_fusion.12) | copy-start | bytes 36868
  139.6 4.9 %copy-start.7 = (s32[24,128]{1,0:T(8,128)S(1)}, s32[24,128]{1,0:T(8,128)}, u32[]{:S(2)}) copy-start(s32[24,128]{1,0:T(8,128)} %add_select_fusion.11) | copy-start | bytes 36868
  140.4 4.9 %copy-start.8 = (s32[24,128]{1,0:T(8,128)S(1)}, s32[24,128]{1,0:T(8,128)}, u32[]{:S(2)}) copy-start(s32[24,128]{1,0:T(8,128)} %add_select_fusion.10) | copy-start | bytes 36868
  141.2 4.9 %copy-start.9 = (s32[24,128]{1,0:T(8,128)S(1)}, s32[24,128]{1,0:T(8,128)}, u32[]{:S(2)}) copy-start(s32[24,128]{1,0:T(8,128)} %add_select_fusion.14) | copy-start | bytes 36868
  142.0 4.9 %copy-start.10 = (s32[24,128]{1,0:T(8,128)S(1)}, s32[24,128]{1,0:T(8,128)}, u32[]{:S(2)}) copy-start(s32[24,128]{1,0:T(8,128)} %add_select_fusion.15) | copy-start | bytes 36868
  143.7 6.4 %copy-start.17 = (u32[32]{0:T(128)S(1)}, u32[32]{0:T(128)}, u32[]{:S(2)}) copy-start(u32[32]{0:T(128)} %constant.218) | copy-start | bytes 388
  148.5 6.4 %collective-permute-start.4 = (f32[21,128]{1,0:T(8,128)S(1)}, f32[21,128]{1,0:T(8,128)S(1)}, u32[]{:S(2)}, u32[]{:S(2)}) collective-permute-start(f32[21,128]{1,0:T(8,128)S(1)} %get-tuple-element.38), channel_id=1, source_target_pairs={{0,4},{4,8},{8,12},{12,16},{16,20},{20,24},{24,28},{28,0},{1,5},{5... | collective-permute-start | bytes 32264 | tf_op jit(solution)/shard_map/ppermute | solution.py:28
  151.3 4.7 %collective-permute-start.5 = (f32[21,128]{1,0:T(8,128)S(1)}, f32[21,128]{1,0:T(8,128)S(1)}, u32[]{:S(2)}, u32[]{:S(2)}) collective-permute-start(f32[21,128]{1,0:T(8,128)S(1)} %get-tuple-element.37), channel_id=1, source_target_pairs={{0,28},{4,0},{8,4},{12,8},{16,12},{20,16},{24,20},{28,24},{1,29},{... | collective-permute-start | bytes 32264 | tf_op jit(solution)/shard_map/ppermute | solution.py:28
Sparse Core Ops, SparseCore 0:
  43.3 33.2 all-reduce.2
where the time goes:
time: 174 us
  waiting for transfers between devices  57.4 us (33%)
  matrix products  30.7 us (18%)
  local copies, waits for them, and re-layouts  21.4 us (12%)
  blocking collectives  20.7 us (12%)
  starting transfers between devices  15.8 us (9%)
  between operations  14.4 us (8%)
  other arithmetic  13.5 us (8%)
    psum x1, waiting for transfers between devices, on_device(): whole_band = lax.psum(part_band, 'col')  32.1 us
    ppermute x2, waiting for transfers between devices, with_halo(): lax.ppermute(lax.slice_in_dim(block, block.shape[dim] - width, None, axis...  23.1 us
    dot_general x16, matrix products, on_device(): jnp.einsum('ip,ipq->iq', contrib[:, slot_index], mover, precision=highest)  13.2 us
    gather x4, local copies, waits for them, and re-layouts, on_device(): picked = ext_band[targets[:, slot_index]]  12.9 us
    psum x1, blocking collectives, on_device(): degree = lax.psum(degree_part, 'col') + prior_ridge  10.6 us
    unnamed x1, blocking collectives  10.1 us
    ppermute x2, starting transfers between devices, with_halo(): lax.ppermute(lax.slice_in_dim(block, 0, width, axis=dim), axis, backward)  6.35 us
    dot_general x1, matrix products, on_device(): applied = jnp.einsum('ikxy,iky->ikx', weights, near_rows, precision=highest)  4.97 us
  transfers between devices with their start and end apart: 7, of which 5 were waited for; matrix products, arithmetic and copies ran while one was open for 10% of the time, Pallas kernels for 0%

commit v1 on v0

--- a/solution.py
+++ b/solution.py
@@ -73,7 +73,7 @@
     )
     prolong = mask_own[:, :, None] * (own_term + relax_weight * applied / degree[:, None, :])
     part_band = band_form(prolong, own_offsets)
-    whole_band = lax.psum(part_band, "col")
+    whole_band = jnp.sum(lax.all_gather(part_band, "col"), axis=0)
     ext_band = with_halo(whole_band, (("row", 0),), H)
     pick_hot = (
         offsets[..., None] + BAND // 2 == jnp.arange(BAND, dtype=jnp.int32)[None, None, :]

time: 174 us -> 169 us (0.971)
  waiting for transfers between devices: 57.4 us -> 50.1 us
  other arithmetic: 13.5 us -> 17.6 us
  local copies, waits for them, and re-layouts: 21.4 us -> 18.7 us
    psum x1 -> x0, waiting for transfers between devices: 32.1 us -> none  [on_device(): whole_band = lax.psum(part_band, 'col')]
    all_gather x0 -> x1, waiting for transfers between devices: none -> 22.2 us  [on_device(): whole_band = jnp.sum(lax.all_gather(part_band, 'col'), axis=0)]
    reduce_sum x0 -> x1, other arithmetic: none -> 3.13 us  [on_device(): whole_band = jnp.sum(lax.all_gather(part_band, 'col'), axis=0)]
    unnamed x40 -> x36, local copies, waits for them, and re-layouts: 3.59 us -> 1.72 us
  transfers between devices with their start and end apart: 7 -> 7, of which waited for: 5 -> 5; matrix products, arithmetic and copies ran while one was open for 10% -> 9% of each run, Pallas kernels for 0% -> 0%
where the time goes in v1:
time: 169 us; the launch traced here: 168 us
  waiting for transfers between devices  50.1 us (30%)
  matrix products  30.7 us (18%)
  blocking collectives  20.8 us (12%)
  local copies, waits for them, and re-layouts  18.7 us (11%)
  other arithmetic  17.6 us (10%)
  starting transfers between devices  15.8 us (9%)
  between operations  14.4 us (9%)
    ppermute x2, waiting for transfers between devices, with_halo(): lax.ppermute(lax.slice_in_dim(block, block.shape[dim] - width, None, axis...  24.5 us
    all_gather x1, waiting for transfers between devices, on_device(): whole_band = jnp.sum(lax.all_gather(part_band, 'col'), axis=0)  22.2 us
    dot_general x16, matrix products, on_device(): jnp.einsum('ip,ipq->iq', contrib[:, slot_index], mover, precision=highest)  13.2 us
    gather x4, local copies, waits for them, and re-layouts, on_device(): picked = ext_band[targets[:, slot_index]]  12.9 us
    psum x1, blocking collectives, on_device(): degree = lax.psum(degree_part, 'col') + prior_ridge  10.6 us
    unnamed x1, blocking collectives  10.2 us
    ppermute x2, starting transfers between devices, with_halo(): lax.ppermute(lax.slice_in_dim(block, 0, width, axis=dim), axis, backward)  6.35 us
    dot_general x1, matrix products, on_device(): applied = jnp.einsum('ikxy,iky->ikx', weights, near_rows, precision=highest)  4.98 us
  transfers between devices with their start and end apart: 7, of which 5 were waited for; matrix products, arithmetic and copies ran while one was open for 9% of the time, Pallas kernels for 0%

profile of v1, /device:TPU:0, one launch (start us, length us, event | category | flops | bytes accessed | tf_op | source)
XLA Modules:
  0.0 167.9 jit_solution(6025646280545218956)
XLA Ops:
  6.5 0.8 multiply_reduce_fusion
  7.4 0.8 broadcast_divide_fusion
  8.2 3.0 %collective-permute-start = (f32[21,64]{1,0:T(8,128)S(1)}, f32[21,64]{1,0:T(8,128)S(1)}, u32[]{:S(2)}, u32[]{:S(2)}) collective-permute-start(f32[21,64]{1,0:T(8,128)S(1)} %get-tuple-element.39), channel_id=1, source_target_pairs={{0,4},{4,8},{8,12},{12,16},{16,20},{20,24},{24,28},{28,0},{1,5},{5... | collective-permute-start | bytes 16136 | tf_op jit(solution)/shard_map/ppermute | solution.py:18
  11.2 3.1 %collective-permute-start.1 = (f32[21,64]{1,0:T(8,128)S(1)}, f32[21,64]{1,0:T(8,128)S(1)}, u32[]{:S(2)}, u32[]{:S(2)}) collective-permute-start(f32[21,64]{1,0:T(8,128)S(1)} %get-tuple-element.40), channel_id=1, source_target_pairs={{4,0},{8,4},{12,8},{16,12},{20,16},{24,20},{28,24},{0,28},{5,1},{9... | collective-permute-start | bytes 16136 | tf_op jit(solution)/shard_map/ppermute | solution.py:21
  18.0 2.9 %reduce_sum.28 = f32[24,4,64]{2,1,0:T(4,128)S(1)} reduce(f32[24,4,64,64]{3,2,1,0:T(8,128)} %param.9, f32[]{:T(128)} %constant.208.clone.1), dimensions={3}, to_apply=%region_1.2 | reduce | flops 387072 | bytes 1597444 | tf_op jit(solution)/shard_map/ikxy,ik->ix/reduce_sum | solution.py:61
  21.2 10.6 %psum.7 = f32[24,64]{1,0:T(8,128)S(1)} all-reduce(f32[24,64]{1,0:T(8,128)S(1)} %bitcast.242), channel_id=1, replica_groups=mesh['row'=8,'col'=4] {'col'}, use_global_device_ids=true, to_apply=%region_2.3 | all-reduce | flops 1536 | bytes 12288 | tf_op jit(solution)/shard_map/psum | solution.py:62
  32.4 5.0 %fusion.175 = f32[24,4,1,64]{3,2,1,0:T(1,128)S(1)} fusion(f32[24,4,64,1]{2,3,1,0:T(1,128)S(1)} %bitcast.241, f32[24,4,64,64]{3,2,1,0:T(8,128)S(1)} %copy-done), kind=kOutput, calls=%fused_computation.336 | convolution fusion | flops 4718592 | bytes 1622016 | tf_op jit(solution)/shard_map/ikxy,iky->ikx/dot_general | solution.py:69
  37.4 1.8 %fusion.57 = f32[24,64,128]{2,1,0:T(8,128)} fusion(f32[24,4,64]{2,1,0:T(4,128)S(1)} %bitcast.240, s32[24,4]{1,0:T(8,128)S(1)} %copy.19, f32[24,64]{1,0:T(8,128)S(1)} %add.344, f32[24,64]{1,0:T(8,128)S(1)} %broadcast_divide_fusion, f32[4]{0:T(128)S(1)} %compare_select_fusion.5, f32[24,4]{1,0:T(8,128)S(1)} %copy.17), kind=kOutput, calls=%fused_computation.91 | convolution fusion | flops 9480192 | bytes 824080 | tf_op jit(solution)/shard_map/nkx,nkq->nxq/dot_general | solution.py:35
  44.0 22.2 %all-gather.3.cloned.1.call-done = f32[96,64,128]{2,1,0:T(8,128)} async-done(((f32[24,64,128]{2,1,0:T(8,128)}), f32[96,64,128]{2,1,0:T(8,128)}) %all-gather.3.cloned.1.call-update) | async-done | bytes 3145744 | tf_op jit(solution)/shard_map/all_gather | solution.py:76
  66.2 3.1 %reduce_sum.29 = f32[24,64,128]{2,1,0:T(8,128)} reduce(f32[4,24,64,128]{3,2,1,0:T(8,128)} %bitcast.238, f32[]{:T(128)} %constant.208.clone.1), dimensions={0}, to_apply=%region_3.4 | reduce | flops 589824 | bytes 3932164 | tf_op jit(solution)/shard_map/reduce_sum | solution.py:76
  69.3 1.5 fusion.172
  70.8 1.5 collective-permute-start.2
  72.3 3.2 %collective-permute-start.3 = (f32[21,64,128]{2,1,0:T(8,128)S(1)}, f32[21,64,128]{2,1,0:T(8,128)S(1)}, u32[]{:S(2)}, u32[]{:S(2)}) collective-permute-start(f32[21,64,128]{2,1,0:T(8,128)S(1)} %get-tuple-element.36), channel_id=1, source_target_pairs={{4,0},{8,4},{12,8},{16,12},{20,16},{24,20},{28,24},{0,28},{5,1},{9... | collective-permute-start | bytes 2064392 | tf_op jit(solution)/shard_map/ppermute | solution.py:21
  77.6 24.5 %collective-permute-done.2 = f32[21,64,128]{2,1,0:T(8,128)S(1)} collective-permute-done((f32[21,64,128]{2,1,0:T(8,128)S(1)}, f32[21,64,128]{2,1,0:T(8,128)S(1)}, u32[]{:S(2)}, u32[]{:S(2)}) %collective-permute-start.2) | collective-permute-done | bytes 688160 | tf_op jit(solution)/shard_map/ppermute | solution.py:18
  102.1 2.2 %collective-permute-done.3 = f32[21,64,128]{2,1,0:T(8,128)S(1)} collective-permute-done((f32[21,64,128]{2,1,0:T(8,128)S(1)}, f32[21,64,128]{2,1,0:T(8,128)S(1)}, u32[]{:S(2)}, u32[]{:S(2)}) %collective-permute-start.3) | collective-permute-done | bytes 688160 | tf_op jit(solution)/shard_map/ppermute | solution.py:21
  104.3 1.5 pad_maximum_fusion
  105.8 3.2 %gather_fusion.1 = f32[24,64,128]{2,1,0:T(8,128)} fusion(f32[66,64,128]{2,1,0:T(8,128)} %pad_maximum_fusion, s32[1024]{0:T(1024)} %pad_clamp_fusion.3), kind=kCustom, calls=%fused_computation.1 | custom fusion | bytes 1572960 | tf_op jit(solution)/shard_map/gather | solution.py:85
  109.0 3.2 %gather_fusion.2 = f32[24,64,128]{2,1,0:T(8,128)} fusion(f32[66,64,128]{2,1,0:T(8,128)} %pad_maximum_fusion, s32[1024]{0:T(1024)} %pad_clamp_fusion.2), kind=kCustom, calls=%fused_computation.2 | custom fusion | bytes 1572960 | tf_op jit(solution)/shard_map/gather | solution.py:85
  112.3 3.2 %gather_fusion.3 = f32[24,64,128]{2,1,0:T(8,128)} fusion(f32[66,64,128]{2,1,0:T(8,128)} %pad_maximum_fusion, s32[1024]{0:T(1024)} %pad_clamp_fusion.1), kind=kCustom, calls=%fused_computation.3 | custom fusion | bytes 1572960 | tf_op jit(solution)/shard_map/gather | solution.py:85
  115.5 3.2 %gather_fusion.4 = f32[24,64,128]{2,1,0:T(8,128)} fusion(f32[66,64,128]{2,1,0:T(8,128)} %pad_maximum_fusion, s32[1024]{0:T(1024)} %pad_clamp_fusion), kind=kCustom, calls=%fused_computation.4 | custom fusion | bytes 1572960 | tf_op jit(solution)/shard_map/gather | solution.py:85
  118.7 2.1 %fusion = f32[24,64,128]{2,1,0:T(8,128)S(1)} fusion(f32[24,64,128]{2,1,0:T(8,128)} %gather_fusion.1, s32[24,128]{1,0:T(8,128)S(1)} %add_select_fusion.19), kind=kOutput, calls=%fused_computation.26 | convolution fusion | flops 302383104 | bytes 1585152 | tf_op jit(solution)/shard_map/iyp,ipq->iyq/dot_general | solution.py:87
  120.8 0.9 convolution_multiply_fusion.3
  121.9 0.9 fusion.1
  122.9 0.9 fusion.2
  123.8 0.9 fusion.3
  124.7 0.9 fusion.24
  125.7 0.9 fusion.23
  126.8 1.0 fusion.22
  127.8 0.8 fusion.177
  128.6 0.8 fusion.10
  129.4 0.8 fusion.11
  130.2 0.8 fusion.12
  131.0 1.0 fusion.13
  132.1 0.8 fusion.14
  132.9 0.8 fusion.15
  133.7 0.8 fusion.16
  134.5 0.8 fusion.17
  135.3 0.8 fusion.18
  136.2 0.8 fusion.19
  137.0 0.8 fusion.6
  137.8 0.8 fusion.7
  138.6 0.8 fusion.8
  139.4 0.8 fusion.9
  140.3 0.8 fusion.5
  141.1 0.8 fusion.4
  144.2 4.5 %collective-permute-start.5 = (f32[21,128]{1,0:T(8,128)S(1)}, f32[21,128]{1,0:T(8,128)S(1)}, u32[]{:S(2)}, u32[]{:S(2)}) collective-permute-start(f32[21,128]{1,0:T(8,128)S(1)} %get-tuple-element.37), channel_id=1, source_target_pairs={{0,28},{4,0},{8,4},{12,8},{16,12},{20,16},{24,20},{28,24},{1,29},{... | collective-permute-start | bytes 32264 | tf_op jit(solution)/shard_map/ppermute | solution.py:28
  149.3 0.8 collective-permute-done.5
  150.3 10.2 %all-reduce = f32[24,128]{1,0:T(8,128)S(1)} all-reduce(f32[24,128]{1,0:T(8,128)S(1)} %scatter-add.9), channel_id=3, replica_groups=mesh['row'=8,'col'=4] {'col'}, use_global_device_ids=true, to_apply=%region_4.5.clone | all-reduce | flops 3072 | bytes 24576
  (101 shorter events, 14.8 us)
Async XLA Ops:
  6.5 59.6 %all-gather.3.cloned.1.call-start = ((), (), s32[]{:S(2)}) async-start(), calls=%async_computation | async-start | bytes 3932160 | tf_op jit(solution)/shard_map/all_gather | solution.py:76
  8.2 23.6 %collective-permute-start = (f32[21,64]{1,0:T(8,128)S(1)}, f32[21,64]{1,0:T(8,128)S(1)}, u32[]{:S(2)}, u32[]{:S(2)}) collective-permute-start(f32[21,64]{1,0:T(8,128)S(1)} %get-tuple-element.39), channel_id=1, source_target_pairs={{0,4},{4,8},{8,12},{12,16},{16,20},{20,24},{24,28},{28,0},{1,5},{5... | collective-permute-start | bytes 16136 | tf_op jit(solution)/shard_map/ppermute | solution.py:18
  11.2 20.6 %collective-permute-start.1 = (f32[21,64]{1,0:T(8,128)S(1)}, f32[21,64]{1,0:T(8,128)S(1)}, u32[]{:S(2)}, u32[]{:S(2)}) collective-permute-start(f32[21,64]{1,0:T(8,128)S(1)} %get-tuple-element.40), channel_id=1, source_target_pairs={{4,0},{8,4},{12,8},{16,12},{20,16},{24,20},{28,24},{0,28},{5,1},{9... | collective-permute-start | bytes 16136 | tf_op jit(solution)/shard_map/ppermute | solution.py:21
  18.0 13.8 %copy-start.11 = (f32[24,64]{1,0:T(8,128)S(1)}, f32[24,64]{1,0:T(8,128)}, u32[]{:S(2)}) copy-start(f32[24,64]{1,0:T(8,128)} %param.13) | copy-start | bytes 18436
  18.0 14.4 %copy-start = (f32[24,4,64,64]{3,2,1,0:T(8,128)S(1)}, f32[24,4,64,64]{3,2,1,0:T(8,128)}, u32[]{:S(2)}) copy-start(f32[24,4,64,64]{3,2,1,0:T(8,128)} %param.9) | copy-start | bytes 4718596
  69.3 7.5 %copy-start.1 = (f32[24,64,128]{2,1,0:T(8,128)S(1)}, f32[24,64,128]{2,1,0:T(8,128)}, u32[]{:S(2)}) copy-start(f32[24,64,128]{2,1,0:T(8,128)} %reduce_sum.29) | copy-start | bytes 2359300
  70.8 31.4 %collective-permute-start.2 = (f32[21,64,128]{2,1,0:T(8,128)S(1)}, f32[21,64,128]{2,1,0:T(8,128)S(1)}, u32[]{:S(2)}, u32[]{:S(2)}) collective-permute-start(f32[21,64,128]{2,1,0:T(8,128)S(1)} %get-tuple-element.35), channel_id=1, source_target_pairs={{0,4},{4,8},{8,12},{12,16},{16,20},{20,24},{24,28},{28,0},{1,5},{5... | collective-permute-start | bytes 2064392 | tf_op jit(solution)/shard_map/ppermute | solution.py:18
  72.3 32.0 %collective-permute-start.3 = (f32[21,64,128]{2,1,0:T(8,128)S(1)}, f32[21,64,128]{2,1,0:T(8,128)S(1)}, u32[]{:S(2)}, u32[]{:S(2)}) collective-permute-start(f32[21,64,128]{2,1,0:T(8,128)S(1)} %get-tuple-element.36), channel_id=1, source_target_pairs={{4,0},{8,4},{12,8},{16,12},{20,16},{24,20},{28,24},{0,28},{5,1},{9... | collective-permute-start | bytes 2064392 | tf_op jit(solution)/shard_map/ppermute | solution.py:21
  115.5 5.3 %copy-start.13 = (f32[24]{0:T(128)S(1)}, f32[24]{0:T(128)}, u32[]{:S(2)}) copy-start(f32[24]{0:T(128)} %get-tuple-element.61) | copy-start | bytes 292
  120.8 1.1 copy-start.5
  120.8 2.1 %copy-start.4 = (f32[24,64,128]{2,1,0:T(8,128)S(1)}, f32[24,64,128]{2,1,0:T(8,128)}, u32[]{:S(2)}) copy-start(f32[24,64,128]{2,1,0:T(8,128)} %gather_fusion.3) | copy-start | bytes 2359300
  121.9 1.9 %copy-start.3 = (f32[24,64,128]{2,1,0:T(8,128)S(1)}, f32[24,64,128]{2,1,0:T(8,128)}, u32[]{:S(2)}) copy-start(f32[24,64,128]{2,1,0:T(8,128)} %gather_fusion.4) | copy-start | bytes 2359300
  122.8 1.9 %copy-start.15 = (f32[24]{0:T(128)S(1)}, f32[24]{0:T(128)}, u32[]{:S(2)}) copy-start(f32[24]{0:T(128)} %get-tuple-element.60) | copy-start | bytes 292
  124.7 0.9 copy-start.14
  125.6 1.1 copy-start.2
  125.7 1.1 copy-start.12
  132.9 4.9 %copy-start.6 = (s32[24,128]{1,0:T(8,128)S(1)}, s32[24,128]{1,0:T(8,128)}, u32[]{:S(2)}) copy-start(s32[24,128]{1,0:T(8,128)} %add_select_fusion.12) | copy-start | bytes 36868
  133.7 4.9 %copy-start.7 = (s32[24,128]{1,0:T(8,128)S(1)}, s32[24,128]{1,0:T(8,128)}, u32[]{:S(2)}) copy-start(s32[24,128]{1,0:T(8,128)} %add_select_fusion.11) | copy-start | bytes 36868
  134.5 4.9 %copy-start.8 = (s32[24,128]{1,0:T(8,128)S(1)}, s32[24,128]{1,0:T(8,128)}, u32[]{:S(2)}) copy-start(s32[24,128]{1,0:T(8,128)} %add_select_fusion.10) | copy-start | bytes 36868
  135.3 4.9 %copy-start.9 = (s32[24,128]{1,0:T(8,128)S(1)}, s32[24,128]{1,0:T(8,128)}, u32[]{:S(2)}) copy-start(s32[24,128]{1,0:T(8,128)} %add_select_fusion.14) | copy-start | bytes 36868
  136.2 4.9 %copy-start.10 = (s32[24,128]{1,0:T(8,128)S(1)}, s32[24,128]{1,0:T(8,128)}, u32[]{:S(2)}) copy-start(s32[24,128]{1,0:T(8,128)} %add_select_fusion.15) | copy-start | bytes 36868
  137.8 5.2 %copy-start.16 = (u32[32]{0:T(128)S(1)}, u32[32]{0:T(128)}, u32[]{:S(2)}) copy-start(u32[32]{0:T(128)} %constant.218) | copy-start | bytes 388
  142.6 6.4 %collective-permute-start.4 = (f32[21,128]{1,0:T(8,128)S(1)}, f32[21,128]{1,0:T(8,128)S(1)}, u32[]{:S(2)}, u32[]{:S(2)}) collective-permute-start(f32[21,128]{1,0:T(8,128)S(1)} %get-tuple-element.38), channel_id=1, source_target_pairs={{0,4},{4,8},{8,12},{12,16},{16,20},{20,24},{24,28},{28,0},{1,5},{5... | collective-permute-start | bytes 32264 | tf_op jit(solution)/shard_map/ppermute | solution.py:28
  144.2 5.9 %collective-permute-start.5 = (f32[21,128]{1,0:T(8,128)S(1)}, f32[21,128]{1,0:T(8,128)S(1)}, u32[]{:S(2)}, u32[]{:S(2)}) collective-permute-start(f32[21,128]{1,0:T(8,128)S(1)} %get-tuple-element.37), channel_id=1, source_target_pairs={{0,28},{4,0},{8,4},{12,8},{16,12},{20,16},{24,20},{28,24},{1,29},{... | collective-permute-start | bytes 32264 | tf_op jit(solution)/shard_map/ppermute | solution.py:28
Sparse Core Ops, SparseCore 0:
  39.4 26.7 all-gather.2
